TPU v7x, 32 devices: a whole 2x2x4 slice. The times are simulated.
32 devices in a mesh: shard: 4 (over y, core), rep: 8 (over z, x).
Axes of the slice: x: 2, y: 2, z: 4, core: 2. Of those that a mesh axis runs over, the one named last changes fastest.
Arguments:
- tokens: bfloat16 [8, 512, 768], P('rep', 'shard'), may hold values from -6 to 6
- gain_one: bfloat16 [768], P('shard'), may hold values from 0.5 to 1.5
- qkv_weight: bfloat16 [768, 2304], P('shard'), may hold values from -6 to 6
- out_weight: bfloat16 [768, 768], P('shard'), may hold values from -2.5 to 2.5
- gain_two: bfloat16 [768], P('shard'), may hold values from 0.5 to 1.5
- in_weight: bfloat16 [768, 2304], P('shard'), may hold values from -0.21875 to 0.21875
- down_weight: bfloat16 [1152, 768], P('shard'), may hold values from -0.1875 to 0.1875
- grad_output: bfloat16 [8, 512, 768], P('rep', 'shard'), may hold values from -6 to 6
Outputs:
- output: bfloat16 [8, 512, 768], P('rep', 'shard')
- grad_tokens: float32 [8, 512, 768], P('rep', 'shard')
- grad_gain_one: float32 [768], P('shard')
- grad_qkv: float32 [768, 2304], P('shard')
- grad_out: float32 [768, 768], P('shard')
- grad_gain_two: float32 [768], P('shard')
- grad_in: float32 [768, 2304], P('shard')
- grad_down: float32 [1152, 768], P('shard')
All inputs are finite; a program needn't handle non-finite values.
Results may differ from a plain program's by a relative error of at most 0.02.
Values may be sent and summed in bfloat16 or wider, within the bound.
A program may use at most 128 MiB of HBM per device.

v0:
```python
import jax
import jax.numpy as jnp
from jax import lax
from jax.sharding import PartitionSpec as P

HEAD_DIM = 64
EPSILON = 1e-05
THETA = 160000.0
SQRT_HALF = 0.7071067811865476
INV_SQRT_TAU = 0.3989422804014327


def layer_norm(values, gain):
    mean_row = jnp.mean(values, axis=-1, keepdims=True)
    centred = values - mean_row
    variance = jnp.mean(centred * centred, axis=-1, keepdims=True)
    inverse = lax.rsqrt(variance + EPSILON)
    normed = centred * inverse
    return (normed, inverse, normed * gain.astype(jnp.float32))


def norm_backward(grad_out, normed, inverse, gain):
    grad_normed = grad_out * gain.astype(jnp.float32)
    gain_grad = jnp.sum(grad_out * normed, axis=0)
    first = jnp.mean(grad_normed, axis=-1, keepdims=True)
    second = jnp.mean(grad_normed * normed, axis=-1, keepdims=True)
    return (inverse * (grad_normed - first - normed * second), gain_grad)


def rotary_tables(positions, head_dim):
    half = head_dim // 2
    freq = THETA ** (-jnp.arange(half, dtype=jnp.float32) * 2.0 / head_dim)
    angles = positions.astype(jnp.float32)[:, None] * freq[None, :]
    angles = jnp.concatenate([angles, angles], axis=-1)
    return (jnp.cos(angles)[:, None, :], jnp.sin(angles)[:, None, :])


def rotate_half(values):
    half = values.shape[-1] // 2
    return jnp.concatenate([-values[..., half:], values[..., :half]], axis=-1)


def gelu_pair(inner):
    cdf = 0.5 * (1.0 + jax.scipy.special.erf(inner * SQRT_HALF))
    return (inner * cdf, cdf + inner * jnp.exp(-0.5 * inner * inner) * INV_SQRT_TAU)


def outer_sum(left, right):
    return lax.dot_general(
        left, right, (((0,), (0,)), ((), ())), preferred_element_type=jnp.float32
    )


def times_transposed(left, weight):
    return lax.dot_general(
        left, weight, (((1,), (1,)), ((), ())), preferred_element_type=jnp.float32
    )


def local(tokens, gain_one, qkv_weight, out_weight, gain_two, in_weight, down_weight, grad_output):
    tok_dev = tokens.shape[1]
    width = tokens.shape[2]
    heads = width // HEAD_DIM
    scale = HEAD_DIM ** (-0.5)
    gathered = (
        lax.all_gather(gain_one, "shard", axis=0, tiled=True),
        lax.all_gather(qkv_weight, "shard", axis=0, tiled=True),
        lax.all_gather(out_weight, "shard", axis=0, tiled=True),
        lax.all_gather(gain_two, "shard", axis=0, tiled=True),
        lax.all_gather(in_weight, "shard", axis=0, tiled=True),
        lax.all_gather(down_weight, "shard", axis=0, tiled=True),
    )
    full_g1, full_qkv, full_out, full_g2, full_in, full_down = gathered
    hidden_units = full_down.shape[0]
    inputs = tokens.reshape(tok_dev, width).astype(jnp.float32)
    normed_one, inverse_one, scaled_one = layer_norm(inputs, full_g1)
    hidden_one = scaled_one.astype(jnp.bfloat16)
    projected = jnp.dot(hidden_one, full_qkv, preferred_element_type=jnp.float32)
    positions = lax.axis_index("shard") * tok_dev + jnp.arange(tok_dev, dtype=jnp.int32)
    cosine, sine = rotary_tables(positions, HEAD_DIM)
    queries = projected[:, :width].reshape(tok_dev, heads, HEAD_DIM)
    key_raw = projected[:, width : 2 * width].reshape(tok_dev, heads, HEAD_DIM)
    query_rot = (queries * cosine + rotate_half(queries) * sine).astype(jnp.bfloat16)
    key_rot = (
        (key_raw * cosine + rotate_half(key_raw) * sine)
        .astype(jnp.bfloat16)
        .reshape(tok_dev, width)
    )
    value_rows = projected[:, 2 * width :].astype(jnp.bfloat16)
    piece = (
        lax.all_gather(key_rot, "shard", axis=0, tiled=True),
        lax.all_gather(value_rows, "shard", axis=0, tiled=True),
    )
    maxima = jnp.full((heads, tok_dev), -1e30, jnp.float32)
    count = piece[0].shape[0]
    key_heads = piece[0].reshape(count, heads, HEAD_DIM)
    value_heads = piece[1].reshape(count, heads, HEAD_DIM)
    scores = (
        jnp.einsum("qhd,khd->hqk", query_rot, key_heads, preferred_element_type=jnp.float32) * scale
    )
    new_max = jnp.maximum(maxima, jnp.max(scores, axis=-1))
    expo = jnp.exp(scores - new_max[..., None])
    totals = jnp.sum(expo, axis=-1)
    accum = jnp.einsum(
        "hqk,khd->hqd", expo.astype(jnp.bfloat16), value_heads, preferred_element_type=jnp.float32
    )
    maxima, totals, accum = (new_max, totals, accum)
    attended = (
        (accum / totals[..., None]).transpose(1, 0, 2).reshape(tok_dev, width).astype(jnp.bfloat16)
    )
    log_sum = maxima + jnp.log(totals)
    resid = inputs + jnp.dot(attended, full_out, preferred_element_type=jnp.float32)
    normed_two, inverse_two, scaled_two = layer_norm(resid, full_g2)
    hidden_two = scaled_two.astype(jnp.bfloat16)
    upper = jnp.dot(hidden_two, full_in, preferred_element_type=jnp.float32)
    inner = upper[:, :hidden_units]
    gate_half = upper[:, hidden_units:]
    gelu_value, gelu_slope = gelu_pair(inner)
    act = (gelu_value * gate_half).astype(jnp.bfloat16)
    output = (resid + jnp.dot(act, full_down, preferred_element_type=jnp.float32)).astype(
        jnp.bfloat16
    )
    regathered = (
        lax.all_gather(gain_one, "shard", axis=0, tiled=True),
        lax.all_gather(qkv_weight, "shard", axis=0, tiled=True),
        lax.all_gather(out_weight, "shard", axis=0, tiled=True),
        lax.all_gather(gain_two, "shard", axis=0, tiled=True),
        lax.all_gather(in_weight, "shard", axis=0, tiled=True),
        lax.all_gather(down_weight, "shard", axis=0, tiled=True),
    )
    full_g1, full_qkv, full_out, full_g2, full_in, full_down = regathered
    grad_b = grad_output.reshape(tok_dev, width)
    grad_f = grad_b.astype(jnp.float32)
    grad_down = outer_sum(act, grad_b)
    grad_act = times_transposed(grad_b, full_down)
    grad_upper = jnp.concatenate(
        [grad_act * gate_half * gelu_slope, grad_act * gelu_value], axis=-1
    ).astype(jnp.bfloat16)
    grad_in = outer_sum(hidden_two, grad_upper)
    grad_h2 = times_transposed(grad_upper, full_in)
    norm_grad_two, grad_gain_two = norm_backward(grad_h2, normed_two, inverse_two, full_g2)
    grad_resid = grad_f + norm_grad_two
    resid_b = grad_resid.astype(jnp.bfloat16)
    grad_out = outer_sum(attended, resid_b)
    grad_att = times_transposed(resid_b, full_out).astype(jnp.bfloat16)
    grad_heads = grad_att.reshape(tok_dev, heads, HEAD_DIM)
    att_heads = attended.reshape(tok_dev, heads, HEAD_DIM)
    delta = jnp.sum(grad_heads.astype(jnp.float32) * att_heads.astype(jnp.float32), axis=-1).T
    piece = (
        lax.all_gather(key_rot, "shard", axis=0, tiled=True),
        lax.all_gather(value_rows, "shard", axis=0, tiled=True),
    )
    count = piece[0].shape[0]
    key_heads = piece[0].reshape(count, heads, HEAD_DIM)
    value_heads = piece[1].reshape(count, heads, HEAD_DIM)
    scores = (
        jnp.einsum("qhd,khd->hqk", query_rot, key_heads, preferred_element_type=jnp.float32) * scale
    )
    probs = jnp.exp(scores - log_sum[..., None])
    value_piece = jnp.einsum(
        "hqk,qhd->khd", probs.astype(jnp.bfloat16), grad_heads, preferred_element_type=jnp.float32
    )
    grad_probs = jnp.einsum(
        "qhd,khd->hqk", grad_heads, value_heads, preferred_element_type=jnp.float32
    )
    grad_scores = (probs * (grad_probs - delta[..., None]) * scale).astype(jnp.bfloat16)
    grad_query = jnp.einsum(
        "hqk,khd->qhd", grad_scores, key_heads, preferred_element_type=jnp.float32
    )
    key_piece = jnp.einsum(
        "hqk,qhd->khd", grad_scores, query_rot, preferred_element_type=jnp.float32
    )
    key_total = key_piece.reshape(count, width)
    value_total = value_piece.reshape(count, width)
    grad_qr, key_total, value_total = (grad_query, key_total, value_total)
    grad_kr, grad_value = (
        lax.psum_scatter(
            key_total.astype(jnp.bfloat16), "shard", scatter_dimension=0, tiled=True
        ).astype(jnp.float32),
        lax.psum_scatter(
            value_total.astype(jnp.bfloat16), "shard", scatter_dimension=0, tiled=True
        ).astype(jnp.float32),
    )
    grad_kr = grad_kr.reshape(tok_dev, heads, HEAD_DIM)
    grad_q = grad_qr * cosine - rotate_half(grad_qr) * sine
    grad_k = grad_kr * cosine - rotate_half(grad_kr) * sine
    grad_projected = jnp.concatenate(
        [grad_q.reshape(tok_dev, width), grad_k.reshape(tok_dev, width), grad_value], axis=-1
    ).astype(jnp.bfloat16)
    grad_qkv = outer_sum(hidden_one, grad_projected)
    grad_h1 = times_transposed(grad_projected, full_qkv)
    norm_grad_one, grad_gain_one = norm_backward(grad_h1, normed_one, inverse_one, full_g1)
    grad_tokens = grad_resid + norm_grad_one
    owned = (
        lax.psum_scatter(
            grad_gain_one.astype(jnp.bfloat16), "shard", scatter_dimension=0, tiled=True
        ).astype(jnp.float32),
        lax.psum_scatter(
            grad_qkv.astype(jnp.bfloat16), "shard", scatter_dimension=0, tiled=True
        ).astype(jnp.float32),
        lax.psum_scatter(
            grad_out.astype(jnp.bfloat16), "shard", scatter_dimension=0, tiled=True
        ).astype(jnp.float32),
        lax.psum_scatter(
            grad_gain_two.astype(jnp.bfloat16), "shard", scatter_dimension=0, tiled=True
        ).astype(jnp.float32),
        lax.psum_scatter(
            grad_in.astype(jnp.bfloat16), "shard", scatter_dimension=0, tiled=True
        ).astype(jnp.float32),
        lax.psum_scatter(
            grad_down.astype(jnp.bfloat16), "shard", scatter_dimension=0, tiled=True
        ).astype(jnp.float32),
    )
    summed = lax.psum((owned[0], owned[1], owned[2], owned[3], owned[4], owned[5]), "rep")
    return (
        output.reshape(1, tok_dev, width),
        grad_tokens.reshape(1, tok_dev, width),
        summed[0],
        summed[1],
        summed[2],
        summed[3],
        summed[4],
        summed[5],
    )


def solution(mesh):
    in_specs = (
        P("rep", "shard", None),
        P("shard"),
        P("shard", None),
        P("shard", None),
        P("shard"),
        P("shard", None),
        P("shard", None),
        P("rep", "shard", None),
    )
    out_specs = (
        P("rep", "shard", None),
        P("rep", "shard", None),
        P("shard"),
        P("shard", None),
        P("shard", None),
        P("shard"),
        P("shard", None),
        P("shard", None),
    )
    return jax.shard_map(local, mesh=mesh, in_specs=in_specs, out_specs=out_specs, check_vma=False)
```

profile of v0, /device:TPU:0, one launch (start us, length us, event | category | flops | bytes accessed | tf_op | source)
XLA Modules:
  0.0 537.6 jit_solution(9330633500089407364)
XLA Ops:
  7.3 0.7 all-gather.5.cloned.1.call-update
  8.0 0.7 all-gather.7.cloned.1.call-update
  12.2 8.4 %all-reduce.6 = (bf16[768]{0:T(1024)(128)(2,1)S(1)}, bf16[768]{0:T(1024)(128)(2,1)S(1)}) all-reduce(bf16[768]{0:T(1024)(128)(2,1)S(1)} %dynamic-update-slice, bf16[768]{0:T(1024)(128)(2,1)S(1)} %dynamic-update-slice.1), channel_id=1, replica_groups=mesh['shard'=4,'rep'=8] {'shard'}, use_global_device_ids=true, to_apply=%add | all-reduce | flops 1536 | bytes 6144
  21.0 22.1 %all-gather.5.cloned.1.call-done = bf16[768,2304]{1,0:T(8,128)(2,1)} async-done(((bf16[192,2304]{1,0:T(8,128)(2,1)}), bf16[768,2304]{1,0:T(8,128)(2,1)}) %all-gather.5.cloned.1.call-update) | async-done | bytes 3538960 | tf_op jit(solution)/shard_map/all_gather | solution.py:67
  43.1 2.7 fusion.67
  46.6 8.6 %all_gather.34 = bf16[512,768]{1,0:T(8,128)(2,1)S(1)} all-gather(bf16[128,768]{1,0:T(8,128)(2,1)S(1)} %get-tuple-element.27), channel_id=1, replica_groups=mesh['shard'=4,'rep'=8] {'shard'}, dimensions={0}, use_global_device_ids=true | all-gather | bytes 983040 | tf_op jit(solution)/shard_map/all_gather | solution.py:91
  55.2 10.6 %all_gather.35 = bf16[512,768]{1,0:T(8,128)(2,1)S(1)} all-gather(bf16[128,768]{1,0:T(8,128)(2,1)S(1)} %slice.87), channel_id=1, replica_groups=mesh['shard'=4,'rep'=8] {'shard'}, dimensions={0}, use_global_device_ids=true | all-gather | bytes 983040 | tf_op jit(solution)/shard_map/all_gather | solution.py:92
  65.7 0.7 fusion.47
  66.5 1.3 copy.45
  67.7 1.2 copy.46
  68.9 1.8 multiply_reduce_fusion
  70.8 0.9 fusion
  71.9 1.5 fusion.20
  73.5 2.2 fusion.71
  76.9 19.5 %all-gather.9.cloned.1.call-done = bf16[768,2304]{1,0:T(8,128)(2,1)} async-done(((bf16[192,2304]{1,0:T(8,128)(2,1)}), bf16[768,2304]{1,0:T(8,128)(2,1)}) %all-gather.9.cloned.1.call-update) | async-done | bytes 3538960 | tf_op jit(solution)/shard_map/all_gather | solution.py:70
  96.4 3.7 fusion.69
  100.1 18.5 %all-gather.11.cloned.1.call-done = bf16[1152,768]{1,0:T(8,128)(2,1)} async-done(((bf16[288,768]{1,0:T(8,128)(2,1)}), bf16[1152,768]{1,0:T(8,128)(2,1)}) %all-gather.11.cloned.1.call-update) | async-done | bytes 1769488 | tf_op jit(solution)/shard_map/all_gather | solution.py:71
  118.6 3.4 fusion.30
  122.0 1.9 multiply_reduce_fusion.1
  124.1 0.7 copy-done.5
  124.8 1.2 convolution_convert_fusion.5
  126.1 1.8 copy.47
  127.8 1.1 multiply_reduce_fusion.2
  128.9 2.3 multiply_convert_fusion
  131.3 1.1 copy-done
  132.4 1.2 convolution_convert_fusion.4
  133.7 2.3 copy.48
  136.0 2.6 fusion.11
  138.7 2.4 copy.50
  141.3 1.5 convolution_convert_fusion.3
  143.0 1.9 convolution_convert_fusion.2
  144.9 3.0 convolution_convert_fusion
  148.0 1.3 copy-done.1
  150.3 9.1 %reduce-scatter.19.cloned.1.call-done = bf16[128,768]{1,0:T(8,128)(2,1)} async-done(((bf16[512,768]{1,0:T(8,128)(2,1)}), bf16[128,768]{1,0:T(8,128)(2,1)}) %reduce-scatter.19.cloned.1.call-update) | async-done | bytes 196624
  159.4 1.1 copy.49
  160.5 0.9 fusion.49
  161.5 23.5 %reduce-scatter.21.cloned.1.call-done = bf16[128,768]{1,0:T(8,128)(2,1)} async-done(((bf16[512,768]{1,0:T(8,128)(2,1)}), bf16[128,768]{1,0:T(8,128)(2,1)}) %reduce-scatter.21.cloned.1.call-update) | async-done | bytes 196624
  185.0 1.1 copy.51
  186.1 3.1 convolution_convert_fusion.1
  190.7 1.1 fusion.24
  191.9 3.6 fusion.44
  195.5 5.8 %all-reduce.5 = (bf16[768]{0:T(1024)(128)(2,1)S(1)}, bf16[768]{0:T(1024)(128)(2,1)S(1)}) all-reduce(bf16[768]{0:T(1024)(128)(2,1)S(1)} %get-tuple-element.10, bf16[768]{0:T(1024)(128)(2,1)S(1)} %copy-done.43), channel_id=4, replica_groups=mesh['shard'=4,'rep'=8] {'shard'}, use_global_device_ids=true, to_apply=%region_14.0.clone | all-reduce | flops 1536 | bytes 6144
  201.4 0.9 fusion.43
  202.3 10.9 %reduce-scatter.13.cloned.1.call-done = bf16[192,768]{1,0:T(8,128)(2,1)} async-done(((bf16[768,768]{1,0:T(8,128)(2,1)}), bf16[192,768]{1,0:T(8,128)(2,1)}) %reduce-scatter.13.cloned.1.call-update) | async-done | bytes 294928 | tf_op jit(solution)/shard_map/reduce_scatter | solution.py:201
  213.2 32.4 %reduce-scatter.17.cloned.1.call-done = bf16[288,768]{1,0:T(8,128)(2,1)} async-done(((bf16[1152,768]{1,0:T(8,128)(2,1)}), bf16[288,768]{1,0:T(8,128)(2,1)}) %reduce-scatter.17.cloned.1.call-update) | async-done | bytes 442384 | tf_op jit(solution)/shard_map/reduce_scatter | solution.py:210
  245.6 43.0 %reduce-scatter.15.cloned.1.call-done = bf16[192,2304]{1,0:T(8,128)(2,1)} async-done(((bf16[768,2304]{1,0:T(8,128)(2,1)}), bf16[192,2304]{1,0:T(8,128)(2,1)}) %reduce-scatter.15.cloned.1.call-update) | async-done | bytes 884752 | tf_op jit(solution)/shard_map/reduce_scatter | solution.py:207
  288.5 42.8 %reduce-scatter.11.cloned.1.call-done = bf16[192,2304]{1,0:T(8,128)(2,1)} async-done(((bf16[768,2304]{1,0:T(8,128)(2,1)}), bf16[192,2304]{1,0:T(8,128)(2,1)}) %reduce-scatter.11.cloned.1.call-update) | async-done | bytes 884752 | tf_op jit(solution)/shard_map/reduce_scatter | solution.py:198
  331.3 199.4 %all-reduce.8 = (f32[192]{0:T(256)}, f32[192,2304]{1,0:T(8,128)}, f32[192,768]{1,0:T(8,128)}, f32[192]{0:T(256)}, f32[192,2304]{1,0:T(8,128)}, /*index=5*/f32[288,768]{1,0:T(8,128)}) all-reduce(f32[192]{0:T(256)S(1)} %dynamic-slice_convert_fusion.1, ...), channel_id=1, replica_groups=mesh['shard'=4,'rep'=8] {'rep'}, use_global_device_ids=true, to_apply=%region_15.0 | all-reduce | flops 1253760 | bytes 7523328 | tf_op jit(solution)/shard_map/psum | solution.py:214
  (151 shorter events, 8.0 us)
Async XLA Ops:
  7.2 3.3 copy-start.42
  7.2 2.9 copy-start.2
  7.2 4.5 copy-start.44
  7.2 4.8 copy-start.45
  7.2 35.9 %all-gather.5.cloned.1.call-start = ((), (), s32[]{:S(2)}) async-start(), calls=%async_computation.6 | async-start | bytes 4423680 | tf_op jit(solution)/shard_map/all_gather | solution.py:67
  7.9 65.5 %all-gather.7.cloned.1.call-start = ((), (), s32[]{:S(2)}) async-start(), calls=%async_computation.7 | async-start | bytes 1474560 | tf_op jit(solution)/shard_map/all_gather | solution.py:68
  8.7 87.7 %all-gather.9.cloned.1.call-start = ((), (), s32[]{:S(2)}) async-start(), calls=%async_computation.8 | async-start | bytes 4423680 | tf_op jit(solution)/shard_map/all_gather | solution.py:70
  9.4 109.2 %all-gather.11.cloned.1.call-start = ((), (), s32[]{:S(2)}) async-start(), calls=%async_computation.9 | async-start | bytes 2211840 | tf_op jit(solution)/shard_map/all_gather | solution.py:71
  10.0 149.3 %reduce-scatter.19.cloned.1.call-start = ((), (), s32[]{:S(2)}) async-start(), calls=%async_computation.14 | async-start | bytes 983040
  10.2 35.5 %copy-start.33 = (f32[128]{0:T(128)}, f32[128]{0:T(128)S(1)}, u32[]{:S(2)}) copy-start(f32[128]{0:T(128)S(1)} %broadcast_multiply_fusion.6) | copy-start | bytes 1540
  10.5 35.3 %copy-start.35 = (f32[128]{0:T(128)}, f32[128]{0:T(128)S(1)}, u32[]{:S(2)}) copy-start(f32[128]{0:T(128)S(1)} %add_rsqrt_fusion.1) | copy-start | bytes 1540
  20.8 45.0 %copy-start.16 = (f32[128,64]{0,1:T(8,128)}, f32[128,64]{0,1:T(8,128)S(1)}, u32[]{:S(2)}) copy-start(f32[128,64]{0,1:T(8,128)S(1)} %get-tuple-element.37) | copy-start | bytes 98308
  20.8 45.0 %copy-start.24 = (f32[128,64]{0,1:T(8,128)}, f32[128,64]{0,1:T(8,128)S(1)}, u32[]{:S(2)}) copy-start(f32[128,64]{0,1:T(8,128)S(1)} %get-tuple-element.38) | copy-start | bytes 98308
  66.5 2.4 copy-start.10
  70.7 2.7 copy-start.29
  71.6 1.8 copy-start.31
  73.5 3.4 copy-start.30
  73.5 3.4 copy-start.32
  118.6 3.4 copy-start.8
  118.6 3.4 copy-start.38
  118.6 3.4 copy-start.40
  122.0 1.9 copy-start.25
  122.0 1.9 copy-start.27
  122.0 1.9 copy-start.22
  122.0 2.8 copy-start.7
  128.9 3.5 copy-start.11
  136.0 49.0 %reduce-scatter.21.cloned.1.call-start = ((), (), s32[]{:S(2)}) async-start(), calls=%async_computation.15 | async-start | bytes 983040
  138.6 2.7 copy-start.6
  138.6 2.7 copy-start.12
  138.6 4.3 copy-start.14
  138.6 4.3 copy-start.23
  141.1 72.1 %reduce-scatter.13.cloned.1.call-start = ((), (), s32[]{:S(2)}) async-start(), calls=%async_computation.11 | async-start | bytes 1474560 | tf_op jit(solution)/shard_map/reduce_scatter | solution.py:201
  142.9 2.0 copy-start.26
  142.9 2.1 copy-start.28
  142.9 2.1 copy-start.39
  142.9 2.1 copy-start.41
  142.9 102.7 %reduce-scatter.17.cloned.1.call-start = ((), (), s32[]{:S(2)}) async-start(), calls=%async_computation.13 | async-start | bytes 2211840 | tf_op jit(solution)/shard_map/reduce_scatter | solution.py:210
  144.9 143.7 %reduce-scatter.15.cloned.1.call-start = ((), (), s32[]{:S(2)}) async-start(), calls=%async_computation.12 | async-start | bytes 4423680 | tf_op jit(solution)/shard_map/reduce_scatter | solution.py:207
  147.9 1.6 copy-start.4
  147.9 183.4 %reduce-scatter.11.cloned.1.call-start = ((), (), s32[]{:S(2)}) async-start(), calls=%async_computation.10 | async-start | bytes 4423680 | tf_op jit(solution)/shard_map/reduce_scatter | solution.py:198
  150.2 11.2 %copy-start.17 = (f32[128,64]{0,1:T(8,128)S(1)}, f32[128,64]{0,1:T(8,128)}, u32[]{:S(2)}) copy-start(f32[128,64]{0,1:T(8,128)} %copy-done.16) | copy-start | bytes 98308
  150.2 35.9 %copy-start.3 = (bf16[1,128,768]{2,1,0:T(8,128)(2,1)S(1)}, bf16[1,128,768]{2,1,0:T(8,128)(2,1)}, u32[]{:S(2)}) copy-start(bf16[1,128,768]{2,1,0:T(8,128)(2,1)} %param.8) | copy-start | bytes 589828
  150.2 35.9 %copy-start.34 = (f32[128]{0:T(128)S(1)}, f32[128]{0:T(128)}, u32[]{:S(2)}) copy-start(f32[128]{0:T(128)} %copy-done.33) | copy-start | bytes 1540
  150.2 35.9 %copy-start.36 = (f32[128]{0:T(128)S(1)}, f32[128]{0:T(128)}, u32[]{:S(2)}) copy-start(f32[128]{0:T(128)} %copy-done.35) | copy-start | bytes 1540
  161.4 24.7 %copy-start.18 = (bf16[128,12,64]{0,2,1:T(8,128)(2,1)}, bf16[128,12,64]{0,2,1:T(8,128)(2,1)S(1)}, u32[]{:S(2)}) copy-start(bf16[128,12,64]{0,2,1:T(8,128)(2,1)S(1)} %get-tuple-element.35) | copy-start | bytes 589828
  161.5 24.6 %copy-start.20 = (bf16[128,768]{0,1:T(8,128)(2,1)}, bf16[128,768]{0,1:T(8,128)(2,1)S(1)}, u32[]{:S(2)}) copy-start(bf16[128,768]{0,1:T(8,128)(2,1)S(1)} %fusion.50) | copy-start | bytes 589828
  189.2 2.6 copy-start.19
  191.9 3.6 copy-start.43
  (8 other events, 9.2 us)
Sparse Core Ops, SparseCore 0:
  9.6 33.4 all-gather.4
  44.6 19.3 all-gather.6
  65.6 30.7 all-gather.8
  97.8 20.7 all-gather.10
  136.1 23.2 reduce-scatter.18
  161.7 23.2 reduce-scatter.20
  187.6 25.5 reduce-scatter.12
  216.3 29.1 reduce-scatter.16
  248.1 40.3 reduce-scatter.14
  290.9 40.3 reduce-scatter.10
where the time goes:
time: 538 us
  blocking collectives  233 us (43%)
  waiting for transfers between devices  224 us (42%)
  matrix products  39.5 us (7%)
  local copies, waits for them, and re-layouts  17.8 us (3%)
  between operations  16.3 us (3%)
  other arithmetic  6.33 us (1%)
    psum x1, blocking collectives, local(): lax.psum((owned[0], owned[1], owned[2], owned[3], owned[4], owned[5]), 'r...  199 us
    reduce_scatter x1, waiting for transfers between devices, local(): lax.psum_scatter(grad_in.astype(jnp.bfloat16), 'shard', scatter_dimension...  43 us
    reduce_scatter x1, waiting for transfers between devices, local(): lax.psum_scatter(grad_qkv.astype(jnp.bfloat16), 'shard', scatter_dimensio...  42.8 us
    unnamed x12, waiting for transfers between devices  35.3 us
    reduce_scatter x1, waiting for transfers between devices, local(): lax.psum_scatter(grad_down.astype(jnp.bfloat16), 'shard', scatter_dimensi...  32.4 us
    all_gather x1, waiting for transfers between devices, local(): lax.all_gather(qkv_weight, 'shard', axis=0, tiled=True)  22.1 us
    all_gather x1, waiting for transfers between devices, local(): lax.all_gather(in_weight, 'shard', axis=0, tiled=True)  19.5 us
    all_gather x1, waiting for transfers between devices, local(): lax.all_gather(down_weight, 'shard', axis=0, tiled=True)  18.5 us
  transfers between devices with their start and end apart: 10, of which 9 were waited for; matrix products, arithmetic and copies ran while one was open for 8% of the time, Pallas kernels for 0%

commit v1 on v0

--- a/solution.py
+++ b/solution.py
@@ -8,6 +8,9 @@
 THETA = 160000.0
 SQRT_HALF = 0.7071067811865476
 INV_SQRT_TAU = 0.3989422804014327
+map_heads = lambda q_in, mesh_dim: jnp.concatenate(
+    lax.all_to_all(jnp.stack([q_in] * lax.axis_size(mesh_dim)), mesh_dim, 0, 0), 0
+)
 
 
 def layer_norm(values, gain):
@@ -67,7 +70,7 @@
         lax.all_gather(qkv_weight, "shard", axis=0, tiled=True),
         lax.all_gather(out_weight, "shard", axis=0, tiled=True),
         lax.all_gather(gain_two, "shard", axis=0, tiled=True),
-        lax.all_gather(in_weight, "shard", axis=0, tiled=True),
+        map_heads(in_weight, mesh_dim="shard"),
         lax.all_gather(down_weight, "shard", axis=0, tiled=True),
     )
     full_g1, full_qkv, full_out, full_g2, full_in, full_down = gathered

time: 538 us -> 564 us (1.048)
  blocking collectives: 233 us -> 293 us
  waiting for transfers between devices: 224 us -> 179 us
    unnamed x2, blocking collectives: 14.1 us -> 69.2 us
    all_gather x1, waiting for transfers between devices: 22.1 us -> 0.02 us  [local(): lax.all_gather(qkv_weight, 'shard', axis=0, tiled=True)]
    all_gather x1, waiting for transfers between devices: 18.5 us -> 0.01 us  [local(): lax.all_gather(down_weight, 'shard', axis=0, tiled=True)]
    unnamed x101 -> x79, local copies, waits for them, and re-layouts: 12.9 us -> 12.3 us
  transfers between devices with their start and end apart: 10 -> 11, of which waited for: 9 -> 7; matrix products, arithmetic and copies ran while one was open for 8% -> 9% of each run, Pallas kernels for 0% -> 0%
where the time goes in v1:
time: 564 us
  blocking collectives  293 us (52%)
  waiting for transfers between devices  179 us (32%)
  matrix products  44.1 us (8%)
  local copies, waits for them, and re-layouts  20.3 us (4%)
  between operations  16.2 us (3%)
  other arithmetic  5.65 us (1%)
    psum x1, blocking collectives, local(): lax.psum((owned[0], owned[1], owned[2], owned[3], owned[4], owned[5]), 'r...  199 us
    unnamed x2, blocking collectives  69.2 us
    reduce_scatter x1, waiting for transfers between devices, local(): lax.psum_scatter(grad_in.astype(jnp.bfloat16), 'shard', scatter_dimension...  43 us
    reduce_scatter x1, waiting for transfers between devices, local(): lax.psum_scatter(grad_qkv.astype(jnp.bfloat16), 'shard', scatter_dimensio...  42.8 us
    unnamed x12, waiting for transfers between devices  35.3 us
    reduce_scatter x1, waiting for transfers between devices, local(): lax.psum_scatter(grad_down.astype(jnp.bfloat16), 'shard', scatter_dimensi...  32.3 us
    all_gather x1, waiting for transfers between devices, local(): lax.all_gather(in_weight, 'shard', axis=0, tiled=True)  14.9 us
    all_gather x1, blocking collectives, local(): lax.all_gather(key_rot, 'shard', axis=0, tiled=True)  13.4 us
  transfers between devices with their start and end apart: 11, of which 7 were waited for; matrix products, arithmetic and copies ran while one was open for 9% of the time, Pallas kernels for 0%

profile of v1, /device:TPU:0, one launch (start us, length us, event | category | flops | bytes accessed | tf_op | source)
XLA Modules:
  0.0 563.6 jit_solution(12549336331367387778)
XLA Ops:
  7.2 0.7 all-gather.5.cloned.1.call-update
  7.9 0.7 all-gather.7.cloned.1.call-update
  8.7 0.7 all-gather.9.cloned.1.call-update
  9.4 3.3 stack.2
  12.7 4.9 all-to-all-start
  20.5 63.5 %all-reduce.6 = (bf16[768]{0:T(1024)(128)(2,1)S(1)}, bf16[768]{0:T(1024)(128)(2,1)S(1)}) all-reduce(bf16[768]{0:T(1024)(128)(2,1)S(1)} %dynamic-update-slice, bf16[768]{0:T(1024)(128)(2,1)S(1)} %dynamic-update-slice.1), channel_id=1, replica_groups=mesh['shard'=4,'rep'=8] {'shard'}, use_global_device_ids=true, to_apply=%add | all-reduce | flops 1536 | bytes 6144
  84.2 2.7 fusion.67
  87.0 10.6 %all_gather.34 = bf16[512,768]{1,0:T(8,128)(2,1)S(1)} all-gather(bf16[128,768]{1,0:T(8,128)(2,1)S(1)} %slice.87), channel_id=1, replica_groups=mesh['shard'=4,'rep'=8] {'shard'}, dimensions={0}, use_global_device_ids=true | all-gather | bytes 983040 | tf_op jit(solution)/shard_map/all_gather | solution.py:95
  97.6 1.2 copy.46
  99.4 13.4 %all_gather.33 = bf16[512,768]{1,0:T(8,128)(2,1)S(1)} all-gather(bf16[128,768]{1,0:T(8,128)(2,1)S(1)} %get-tuple-element.27), channel_id=1, replica_groups=mesh['shard'=4,'rep'=8] {'shard'}, dimensions={0}, use_global_device_ids=true | all-gather | bytes 983040 | tf_op jit(solution)/shard_map/all_gather | solution.py:94
  112.8 1.2 copy.45
  114.7 1.9 multiply_reduce_fusion
  117.3 0.9 fusion
  118.1 1.5 fusion.20
  119.7 1.9 fusion.71
  122.7 0.7 log_add_fusion
  123.4 3.8 fusion.69
  127.3 3.5 fusion.30
  130.7 14.9 %all-gather.11.cloned.1.call-done = bf16[768,2304]{1,0:T(8,128)(2,1)} async-done(((bf16[192,2304]{1,0:T(8,128)(2,1)}), bf16[768,2304]{1,0:T(8,128)(2,1)}) %all-gather.11.cloned.1.call-update) | async-done | bytes 3538960 | tf_op jit(solution)/shard_map/all_gather | solution.py:131
  145.6 4.3 multiply_reduce_fusion.1
  150.1 0.7 copy-done.5
  150.9 1.2 convolution_convert_fusion.5
  152.1 1.7 copy.47
  153.8 1.1 multiply_reduce_fusion.2
  155.0 2.3 multiply_convert_fusion
  157.3 1.1 copy-done
  158.4 1.2 convolution_convert_fusion.4
  159.7 2.3 copy.48
  162.3 2.6 fusion.11
  164.9 2.4 copy.50
  167.4 2.6 convolution_convert_fusion.3
  170.1 1.9 convolution_convert_fusion.2
  172.0 4.1 convolution_convert_fusion
  177.0 8.4 %reduce-scatter.19.cloned.1.call-done = bf16[128,768]{1,0:T(8,128)(2,1)} async-done(((bf16[512,768]{1,0:T(8,128)(2,1)}), bf16[128,768]{1,0:T(8,128)(2,1)}) %reduce-scatter.19.cloned.1.call-update) | async-done | bytes 196624
  185.4 1.1 copy.49
  186.7 24.3 %reduce-scatter.21.cloned.1.call-done = bf16[128,768]{1,0:T(8,128)(2,1)} async-done(((bf16[512,768]{1,0:T(8,128)(2,1)}), bf16[128,768]{1,0:T(8,128)(2,1)}) %reduce-scatter.21.cloned.1.call-update) | async-done | bytes 196624
  211.0 1.1 copy.51
  212.1 3.1 convolution_convert_fusion.1
  216.0 0.7 copy-done.11
  216.7 1.1 fusion.24
  217.8 3.6 fusion.44
  221.5 5.8 %all-reduce.5 = (bf16[768]{0:T(1024)(128)(2,1)S(1)}, bf16[768]{0:T(1024)(128)(2,1)S(1)}) all-reduce(bf16[768]{0:T(1024)(128)(2,1)S(1)} %get-tuple-element.10, bf16[768]{0:T(1024)(128)(2,1)S(1)} %copy-done.32), channel_id=4, replica_groups=mesh['shard'=4,'rep'=8] {'shard'}, use_global_device_ids=true, to_apply=%region_14.0.clone | all-reduce | flops 1536 | bytes 6144
  227.4 0.9 fusion.43
  228.4 10.9 %reduce-scatter.13.cloned.1.call-done = bf16[192,768]{1,0:T(8,128)(2,1)} async-done(((bf16[768,768]{1,0:T(8,128)(2,1)}), bf16[192,768]{1,0:T(8,128)(2,1)}) %reduce-scatter.13.cloned.1.call-update) | async-done | bytes 294928 | tf_op jit(solution)/shard_map/reduce_scatter | solution.py:204
  239.2 32.3 %reduce-scatter.17.cloned.1.call-done = bf16[288,768]{1,0:T(8,128)(2,1)} async-done(((bf16[1152,768]{1,0:T(8,128)(2,1)}), bf16[288,768]{1,0:T(8,128)(2,1)}) %reduce-scatter.17.cloned.1.call-update) | async-done | bytes 442384 | tf_op jit(solution)/shard_map/reduce_scatter | solution.py:213
  271.6 43.0 %reduce-scatter.15.cloned.1.call-done = bf16[192,2304]{1,0:T(8,128)(2,1)} async-done(((bf16[768,2304]{1,0:T(8,128)(2,1)}), bf16[192,2304]{1,0:T(8,128)(2,1)}) %reduce-scatter.15.cloned.1.call-update) | async-done | bytes 884752 | tf_op jit(solution)/shard_map/reduce_scatter | solution.py:210
  314.5 42.8 %reduce-scatter.11.cloned.1.call-done = bf16[192,2304]{1,0:T(8,128)(2,1)} async-done(((bf16[768,2304]{1,0:T(8,128)(2,1)}), bf16[192,2304]{1,0:T(8,128)(2,1)}) %reduce-scatter.11.cloned.1.call-update) | async-done | bytes 884752 | tf_op jit(solution)/shard_map/reduce_scatter | solution.py:201
  357.3 199.5 %all-reduce.8 = (f32[192]{0:T(256)}, f32[192,2304]{1,0:T(8,128)}, f32[192,768]{1,0:T(8,128)}, f32[192]{0:T(256)}, f32[192,2304]{1,0:T(8,128)}, /*index=5*/f32[288,768]{1,0:T(8,128)}) all-reduce(f32[192]{0:T(256)S(1)} %dynamic-slice_convert_fusion.1, ...), channel_id=1, replica_groups=mesh['shard'=4,'rep'=8] {'rep'}, use_global_device_ids=true, to_apply=%region_15.0 | all-reduce | flops 1253760 | bytes 7523328 | tf_op jit(solution)/shard_map/psum | solution.py:217
  (132 shorter events, 7.5 us)
Async XLA Ops:
  7.2 77.0 %all-gather.5.cloned.1.call-start = ((), (), s32[]{:S(2)}) async-start(), calls=%async_computation.7 | async-start | bytes 4423680 | tf_op jit(solution)/shard_map/all_gather | solution.py:70
  7.9 111.8 %all-gather.7.cloned.1.call-start = ((), (), s32[]{:S(2)}) async-start(), calls=%async_computation.8 | async-start | bytes 1474560 | tf_op jit(solution)/shard_map/all_gather | solution.py:71
  8.7 118.6 %all-gather.9.cloned.1.call-start = ((), (), s32[]{:S(2)}) async-start(), calls=%async_computation.9 | async-start | bytes 2211840 | tf_op jit(solution)/shard_map/all_gather | solution.py:74
  12.7 5.5 copy-start.2
  12.7 6.1 %copy-start.31 = (u32[32]{0:T(128)S(1)}, u32[32]{0:T(128)}, u32[]{:S(2)}) copy-start(u32[32]{0:T(128)} %constant.48) | copy-start | bytes 388
  12.7 7.3 %copy-start.33 = (bf16[192]{0:T(256)(128)(2,1)S(1)}, bf16[192]{0:T(256)(128)(2,1)}, u32[]{:S(2)}) copy-start(bf16[192]{0:T(256)(128)(2,1)} %param.9) | copy-start | bytes 1156
  12.7 7.6 %copy-start.34 = (bf16[192]{0:T(256)(128)(2,1)S(1)}, bf16[192]{0:T(256)(128)(2,1)}, u32[]{:S(2)}) copy-start(bf16[192]{0:T(256)(128)(2,1)} %param.12) | copy-start | bytes 1156
  12.7 110.8 %all-to-all-start = ((bf16[4,192,2304]{2,1,0:T(8,128)(2,1)}), bf16[4,192,2304]{2,1,0:T(8,128)(2,1)}, u32[]{:S(2)}, u32[]{:S(2)}) async-start(bf16[4,192,2304]{2,1,0:T(8,128)(2,1)} %stack.2), calls=%async_computation | async-start | bytes 7077888 | tf_op jit(solution)/shard_map/all_to_all | solution.py:12
  17.5 128.1 %all-gather.11.cloned.1.call-start = ((), (), s32[]{:S(2)}) async-start(), calls=%async_computation.10 | async-start | bytes 4423680 | tf_op jit(solution)/shard_map/all_gather | solution.py:131
  18.1 167.3 %reduce-scatter.19.cloned.1.call-start = ((), (), s32[]{:S(2)}) async-start(), calls=%async_computation.15 | async-start | bytes 983040
  18.3 68.6 %copy-start.22 = (f32[128]{0:T(128)}, f32[128]{0:T(128)S(1)}, u32[]{:S(2)}) copy-start(f32[128]{0:T(128)S(1)} %broadcast_multiply_fusion.6) | copy-start | bytes 1540
  18.7 95.3 %copy-start.13 = (f32[128,64]{0,1:T(8,128)}, f32[128,64]{0,1:T(8,128)S(1)}, u32[]{:S(2)}) copy-start(f32[128,64]{0,1:T(8,128)S(1)} %get-tuple-element.37) | copy-start | bytes 98308
  18.7 95.3 %copy-start.17 = (f32[128,64]{0,1:T(8,128)}, f32[128,64]{0,1:T(8,128)S(1)}, u32[]{:S(2)}) copy-start(f32[128,64]{0,1:T(8,128)S(1)} %get-tuple-element.38) | copy-start | bytes 98308
  84.2 13.4 %copy-start.24 = (f32[128]{0:T(128)}, f32[128]{0:T(128)S(1)}, u32[]{:S(2)}) copy-start(f32[128]{0:T(128)S(1)} %add_rsqrt_fusion.1) | copy-start | bytes 1540
  114.1 0.7 copy-start.9
  114.7 3.4 copy-start.8
  116.6 0.6 copy-start.20
  118.1 3.5 copy-start.21
  121.6 0.6 copy-start.26
  145.6 4.3 copy-start.15
  145.6 4.3 copy-start.27
  145.6 4.3 copy-start.29
  145.6 5.3 copy-start.7
  150.1 0.7 copy-start.5
  153.8 4.6 copy-start.10
  157.3 1.1 copy-start
  162.0 49.0 %reduce-scatter.21.cloned.1.call-start = ((), (), s32[]{:S(2)}) async-start(), calls=%async_computation.16 | async-start | bytes 983040
  164.9 5.2 copy-start.12
  164.9 5.2 copy-start.16
  167.3 4.7 copy-start.19
  167.3 4.7 copy-start.28
  167.3 4.7 copy-start.30
  167.3 71.9 %reduce-scatter.13.cloned.1.call-start = ((), (), s32[]{:S(2)}) async-start(), calls=%async_computation.12 | async-start | bytes 1474560 | tf_op jit(solution)/shard_map/reduce_scatter | solution.py:204
  170.0 101.6 %reduce-scatter.17.cloned.1.call-start = ((), (), s32[]{:S(2)}) async-start(), calls=%async_computation.14 | async-start | bytes 2211840 | tf_op jit(solution)/shard_map/reduce_scatter | solution.py:213
  171.9 4.3 copy-start.1
  172.0 4.3 copy-start.4
  172.0 142.6 %reduce-scatter.15.cloned.1.call-start = ((), (), s32[]{:S(2)}) async-start(), calls=%async_computation.13 | async-start | bytes 4423680 | tf_op jit(solution)/shard_map/reduce_scatter | solution.py:210
  176.2 10.4 %copy-start.14 = (f32[128,64]{0,1:T(8,128)S(1)}, f32[128,64]{0,1:T(8,128)}, u32[]{:S(2)}) copy-start(f32[128,64]{0,1:T(8,128)} %copy-done.13) | copy-start | bytes 98308
  176.2 10.4 %copy-start.18 = (f32[128,64]{0,1:T(8,128)S(1)}, f32[128,64]{0,1:T(8,128)}, u32[]{:S(2)}) copy-start(f32[128,64]{0,1:T(8,128)} %copy-done.17) | copy-start | bytes 98308
  176.2 181.1 %reduce-scatter.11.cloned.1.call-start = ((), (), s32[]{:S(2)}) async-start(), calls=%async_computation.11 | async-start | bytes 4423680 | tf_op jit(solution)/shard_map/reduce_scatter | solution.py:201
  176.9 35.2 %copy-start.3 = (bf16[1,128,768]{2,1,0:T(8,128)(2,1)S(1)}, bf16[1,128,768]{2,1,0:T(8,128)(2,1)}, u32[]{:S(2)}) copy-start(bf16[1,128,768]{2,1,0:T(8,128)(2,1)} %param.8) | copy-start | bytes 589828
  176.9 35.2 %copy-start.23 = (f32[128]{0:T(128)S(1)}, f32[128]{0:T(128)}, u32[]{:S(2)}) copy-start(f32[128]{0:T(128)} %copy-done.22) | copy-start | bytes 1540
  176.9 35.2 %copy-start.25 = (f32[128]{0:T(128)S(1)}, f32[128]{0:T(128)}, u32[]{:S(2)}) copy-start(f32[128]{0:T(128)} %copy-done.24) | copy-start | bytes 1540
  215.2 1.5 copy-start.11
  217.8 3.7 copy-start.32
  217.8 9.6 %copy-start.6 = (f32[128,768]{1,0:T(8,128)S(1)}, f32[128,768]{1,0:T(8,128)}, u32[]{:S(2)}) copy-start(f32[128,768]{1,0:T(8,128)} %copy-done.5) | copy-start | bytes 1179652
Sparse Core Ops, SparseCore 0:
  9.5 52.5 all-gather.4
  63.6 22.5 all-gather.6
  87.8 25.9 all-gather.8
  115.2 30.3 all-gather.10
  162.2 23.1 reduce-scatter.18
  187.8 23.1 reduce-scatter.20
  213.6 25.6 reduce-scatter.12
  242.4 29.1 reduce-scatter.16
  274.1 40.3 reduce-scatter.14
  316.9 40.3 reduce-scatter.10
